TPU v7x, 32 devices: a whole 2x2x4 slice. The times are simulated.
32 devices in a mesh: dap: 8 (over z, x), head: 4 (over y, core).
Axes of the slice: x: 2, y: 2, z: 4, core: 2. Of those that a mesh axis runs over, the one named last changes fastest.
Arguments:
- multiple_aligned_family: bfloat16 [128, 128, 256], P('dap')
- homolog_present_flags: int32 [128], replicated, may hold values from 0 to 1, as said below
- amino_present_flags: int32 [128], replicated, may hold values 0 or 1
- focus_layernorm_scaling: float32 [256], replicated, may hold values from 0.5 to 1.5
- focus_layernorm_offset: float32 [256], replicated, may hold values from -1.8 to 1.8
- combined_focus_matrices: bfloat16 [256, 4, 256], P(None, None, 'head')
- sigmoid_switch_offset: float32 [256], P('head'), may hold values from -4 to 4
- focus_final_matrix: bfloat16 [256, 256], P('head'), may hold values from -0.375 to 0.375
- focus_final_offset: float32 [256], replicated, may hold values from -3 to 3
- tensor_layernorm_scaling: float32 [256], replicated, may hold values from 0.5 to 1.5
- tensor_layernorm_offset: float32 [256], replicated, may hold values from -1.8 to 1.8
- tensor_product_factors: bfloat16 [256, 2, 32], replicated, may hold values from -0.375 to 0.375
- tensor_final_matrix: float32 [1024, 128], replicated, may hold values from -0.1875 to 0.1875
- tensor_final_offset: float32 [128], replicated, may hold values from -4 to 4
Outputs:
- alignment_output: bfloat16 [128, 128, 256], P(('dap', 'head'))
- pair_mean_update: float32 [128, 128, 128], P('dap', 'head')
Inputs may be any that keep to these rules, and one draw needn't show every extreme that they name: homolog_present_flags[0] is always 1.
All inputs are finite; a program needn't handle non-finite values.
Results may differ from a plain program's by a relative error of at most 0.005.
Values may be sent and summed in bfloat16 or wider, within the bound.
A program may use at most 256 MiB of HBM per device.

v0:
```python
import jax
import jax.numpy as jnp
from jax import lax
from jax.sharding import PartitionSpec as P

DH = 32
CO = 32


def layer_norm(value, gain, bias):
    mean = jnp.mean(value, -1, keepdims=True)
    centred = value - mean
    spread = jnp.mean(centred * centred, -1, keepdims=True)
    return centred * lax.rsqrt(spread + 1e-05) * gain + bias


def attend_column(query, keys, values, gate, keep):
    scores = jnp.einsum("shd,thd->hst", query, keys, preferred_element_type=jnp.float32)
    scores = jnp.where(keep[None, None, :], scores, jnp.float32(-1000000000.0))
    top = jnp.max(scores, -1, keepdims=True)
    weights = jnp.exp(scores - top)
    probs = (weights / jnp.sum(weights, -1, keepdims=True)).astype(jnp.bfloat16)
    mixed = jnp.einsum("hst,thd->shd", probs, values, preferred_element_type=jnp.float32)
    return (mixed * gate).astype(jnp.bfloat16)


def per_device(
    multiple_aligned_family,
    homolog_present_flags,
    amino_present_flags,
    focus_layernorm_scaling,
    focus_layernorm_offset,
    combined_focus_matrices,
    sigmoid_switch_offset,
    focus_final_matrix,
    focus_final_offset,
    tensor_layernorm_scaling,
    tensor_layernorm_offset,
    tensor_product_factors,
    tensor_final_matrix,
    tensor_final_offset,
):
    parallel_devices = lax.axis_size("dap")
    n_head = lax.axis_size("head")
    head_id = lax.axis_index("head")
    dap_id = lax.axis_index("dap")
    homolog_shard_number, amino_total, feature_dimension = multiple_aligned_family.shape
    total_seqs = homolog_present_flags.shape[0]
    residue_device_count = amino_total // parallel_devices
    local_heads = sigmoid_switch_offset.shape[0] // DH
    keep = homolog_present_flags > 0
    weights_in = combined_focus_matrices.reshape(feature_dimension, 4 * local_heads * DH)
    gate_shift = sigmoid_switch_offset.reshape(local_heads, DH)
    bundled_focus_units = multiple_aligned_family.reshape(
        homolog_shard_number, parallel_devices, residue_device_count, feature_dimension
    )
    received = lax.all_to_all(bundled_focus_units, "dap", split_axis=1, concat_axis=0, tiled=True)
    block = received[:, 0]
    count = block.shape[1]
    normed = layer_norm(
        block.astype(jnp.float32), focus_layernorm_scaling, focus_layernorm_offset
    ).astype(jnp.bfloat16)
    projected = jnp.dot(
        normed.reshape(total_seqs * count, feature_dimension),
        weights_in,
        preferred_element_type=jnp.float32,
    )
    projected = projected.reshape(total_seqs, count, 4, local_heads, DH)
    query = jnp.moveaxis((projected[:, :, 0] * DH ** (-0.5)).astype(jnp.bfloat16), 1, 0)
    keys = jnp.moveaxis(projected[:, :, 1].astype(jnp.bfloat16), 1, 0)
    values = jnp.moveaxis(projected[:, :, 2].astype(jnp.bfloat16), 1, 0)
    gate = jnp.moveaxis(jax.nn.sigmoid(projected[:, :, 3] + gate_shift), 1, 0)

    def single(operands):
        return attend_column(operands[0], operands[1], operands[2], operands[3], keep)

    attended = lax.map(single, (query, keys, values, gate))
    attended = jnp.moveaxis(attended, 0, 1).reshape(total_seqs * count, local_heads * DH)
    partial_value = jnp.dot(attended, focus_final_matrix, preferred_element_type=jnp.float32)
    partial_value, columns = (
        partial_value.reshape(total_seqs, 1, count, feature_dimension),
        received,
    )
    group = homolog_shard_number // n_head
    columns = columns.reshape(
        parallel_devices, n_head, group, residue_device_count, feature_dimension
    )
    partial_value = partial_value.reshape(
        parallel_devices, n_head, group, residue_device_count, feature_dimension
    )
    summed = lax.psum(partial_value.astype(jnp.bfloat16), "head").astype(jnp.float32)
    summed_mine = lax.dynamic_index_in_dim(summed, head_id, 1, keepdims=True)
    own = lax.dynamic_index_in_dim(columns, head_id, 1, keepdims=True)
    mine = (own.astype(jnp.float32) + summed_mine + focus_final_offset).astype(jnp.bfloat16)
    alignment_rows = lax.all_to_all(
        mine.reshape(parallel_devices * group, residue_device_count, feature_dimension),
        "dap",
        split_axis=0,
        concat_axis=1,
        tiled=True,
    )
    seq_keep = homolog_present_flags.astype(jnp.float32).reshape(parallel_devices, n_head, group)
    row_keep = lax.dynamic_slice_in_dim(
        amino_present_flags, dap_id * residue_device_count, residue_device_count
    ).astype(jnp.float32)
    stack = mine.reshape(parallel_devices * group, residue_device_count, feature_dimension)
    mask_seq = lax.dynamic_index_in_dim(seq_keep, head_id, 1, keepdims=False).reshape(
        parallel_devices * group
    )
    left_weight = tensor_product_factors[:, 0]
    right_weight = tensor_product_factors[:, 1]
    used = stack.shape[0]
    opm_normed = layer_norm(
        stack.astype(jnp.float32), tensor_layernorm_scaling, tensor_layernorm_offset
    ).astype(jnp.bfloat16)
    flat = opm_normed.reshape(used * residue_device_count, feature_dimension)
    keep_rs = mask_seq[:, None, None] * row_keep[None, :, None]
    left = (
        jnp.dot(flat, left_weight, preferred_element_type=jnp.float32).reshape(
            used, residue_device_count, -1
        )
        * keep_rs
    ).astype(jnp.bfloat16)
    right = (
        jnp.dot(flat, right_weight, preferred_element_type=jnp.float32).reshape(
            used, residue_device_count, CO
        )
        * keep_rs
    ).astype(jnp.bfloat16)
    piece = lax.all_gather(right, "dap", axis=1, tiled=True)
    outer = lax.dot_general(
        left, piece, (((0,), (0,)), ((), ())), preferred_element_type=jnp.float32
    )
    outer = outer.transpose(0, 2, 1, 3).reshape(residue_device_count, piece.shape[1], -1)
    partial_pair = jnp.dot(
        outer,
        tensor_final_matrix,
        precision=lax.Precision.HIGHEST,
        preferred_element_type=jnp.float32,
    )
    pair = lax.psum_scatter(partial_pair, "head", scatter_dimension=1, tiled=True)
    col_width = amino_total // n_head
    col_keep = lax.dynamic_slice_in_dim(amino_present_flags, head_id * col_width, col_width).astype(
        jnp.float32
    )
    count = jnp.sum(homolog_present_flags).astype(jnp.float32)
    norm = jnp.maximum(count * row_keep[:, None] * col_keep[None, :], 1.0)
    pair_mean_update = (pair + tensor_final_offset) / norm[:, :, None]
    return (alignment_rows, pair_mean_update)


def solution(mesh):
    return jax.shard_map(
        per_device,
        mesh=mesh,
        in_specs=(
            P("dap", None, None),
            P(),
            P(),
            P(),
            P(),
            P(None, None, "head"),
            P("head"),
            P("head", None),
            P(),
            P(),
            P(),
            P(),
            P(),
            P(),
        ),
        out_specs=(P(("dap", "head"), None, None), P("dap", "head", None)),
        check_vma=False,
    )
```

profile of v0, /device:TPU:0, one launch (start us, length us, event | category | flops | bytes accessed | tf_op | source)
XLA Modules:
  0.0 189.5 jit_solution(11915135432507252343)
XLA Ops:
  7.2 2.4 %copy.23 = bf16[16,8,16,256]{3,2,0,1:T(8,128)(2,1)} copy(bf16[16,8,16,256]{3,2,1,0:T(8,128)(2,1)} %bitcast.152) | data formatting | bytes 2097152 | tf_op jit(solution)/shard_map/reshape | solution.py:54
  9.6 7.4 %all-to-all-start = ((bf16[16,8,16,256]{3,2,0,1:T(8,128)(2,1)}), bf16[16,8,16,256]{3,2,0,1:T(8,128)(2,1)S(1)}, u32[]{:S(2)}, u32[]{:S(2)}) async-start(bf16[16,8,16,256]{3,2,0,1:T(8,128)(2,1)} %copy.23), calls=%async_computation | async-start | bytes 2097152 | tf_op jit(solution)/shard_map/all_to_all | solution.py:57
  17.1 25.6 %all-to-all-done = bf16[16,8,16,256]{3,2,0,1:T(8,128)(2,1)S(1)} async-done(((bf16[16,8,16,256]{3,2,0,1:T(8,128)(2,1)}), bf16[16,8,16,256]{3,2,0,1:T(8,128)(2,1)S(1)}, u32[]{:S(2)}, u32[]{:S(2)}) %all-to-all-start) | async-done | bytes 1048608 | tf_op jit(solution)/shard_map/all_to_all | solution.py:57
  42.8 0.3 convert_reduce_fusion
  43.1 0.7 fusion.43
  43.8 0.7 fusion.46
  44.6 0.3 copy.24
  44.9 0.5 fusion.79
  45.5 0.2 fusion.59
  45.8 10.6 %while.10 = (s32[]{:T(128)}, bf16[16,128,2,32]{1,3,2,0:T(8,128)(2,1)S(1)}, bf16[16,128,2,32]{1,3,2,0:T(8,128)(2,1)S(1)}, pred[128]{0:T(512)(128)(4,1)S(1)}, bf16...) while((s32[]{:T(128)}, ...), condition=%wide.region_5.6_spmd, body=%wide.region_2.5_spmd.sunk | while | flops 6537728 | bytes 137301 | solution.py:77
  45.8 0.3 fusion.98
  46.0 0.4 fusion.99
  46.4 0.3 fusion.98
  46.7 0.4 fusion.99
  47.1 0.3 fusion.98
  47.4 0.4 fusion.99
  47.8 0.3 fusion.98
  48.0 0.4 fusion.99
  48.4 0.3 fusion.98
  48.7 0.4 fusion.99
  49.1 0.3 fusion.98
  49.4 0.4 fusion.99
  49.7 0.3 fusion.98
  50.0 0.4 fusion.99
  50.4 0.3 fusion.98
  50.7 0.4 fusion.99
  51.1 0.3 fusion.98
  51.3 0.4 fusion.99
  51.7 0.3 fusion.98
  52.0 0.4 fusion.99
  52.4 0.3 fusion.98
  52.7 0.4 fusion.99
  53.1 0.3 fusion.98
  53.3 0.4 fusion.99
  53.7 0.3 fusion.98
  54.0 0.4 fusion.99
  54.4 0.3 fusion.98
  54.7 0.4 fusion.99
  55.0 0.3 fusion.98
  55.3 0.4 fusion.99
  55.7 0.3 fusion.98
  56.0 0.4 fusion.99
  56.4 0.9 copy.25
  57.3 0.5 dot_general.33
  57.9 1.4 convolution_convert_fusion
  59.4 0.6 fusion.78
  60.0 0.1 reshape.285
  61.1 33.8 %all-reduce.2.cloned.1.call-done = bf16[8,4,4,16,256]{4,3,2,1,0:T(8,128)(2,1)} async-done(((bf16[8,4,4,16,256]{4,3,2,1,0:T(8,128)(2,1)}), bf16[8,4,4,16,256]{4,3,2,1,0:T(8,128)(2,1)}) %all-reduce.2.cloned.1.call-update) | async-done | bytes 1048592 | tf_op jit(solution)/shard_map/psum | solution.py:91
  94.8 1.7 convert_reduce_fusion.1
  96.6 1.2 fusion.50
  97.9 1.2 fusion.53
  99.0 0.2 fusion.69
  99.2 0.2 fusion.67
  99.4 0.2 copy.33
  99.6 0.2 copy.34
  99.9 33.2 %all_gather.3 = bf16[32,128,32]{0,1,2:T(8,128)(2,1)S(1)} all-gather(bf16[32,16,32]{0,1,2:T(8,128)(2,1)S(1)} %get-tuple-element.61), channel_id=1, replica_groups=mesh['dap'=8,'head'=4] {'dap'}, dimensions={1}, use_global_device_ids=true | all-gather | bytes 294912 | tf_op jit(solution)/shard_map/all_gather | solution.py:130
  133.1 1.3 convolution_bitcast_fusion.1
  134.3 6.5 %copy.28 = f32[16,128,32,32]{1,3,2,0:T(8,128)S(1)} copy(f32[16,128,32,32]{1,2,3,0:T(8,128)S(1)} %convolution_bitcast_fusion.1) | data formatting | bytes 16777216 | tf_op jit(solution)/shard_map/transpose | solution.py:134
  140.8 14.9 %fusion.61 = f32[16,128,128]{2,1,0:T(8,128)} fusion(f32[16,128,1024]{1,2,0:T(8,128)S(1)} %bitcast.147, f32[1024,128]{1,0:T(8,128)S(1)} %copy-done), kind=kOutput, calls=%fused_computation.52 | convolution fusion | flops 3221225472 | bytes 9961472 | tf_op jit(solution)/shard_map/dot_general | solution.py:135
  155.7 5.4 %all-to-all-start.1 = ((bf16[32,16,256]{2,1,0:T(8,128)(2,1)}), bf16[32,16,256]{2,1,0:T(8,128)(2,1)S(1)}, u32[]{:S(2)}, u32[]{:S(2)}) async-start(bf16[32,16,256]{2,1,0:T(8,128)(2,1)} %bitcast.29), calls=%async_computation.1 | async-start | bytes 524288 | tf_op jit(solution)/shard_map/all_to_all | solution.py:95
  161.2 8.1 %all-to-all-done.1 = bf16[32,16,256]{2,1,0:T(8,128)(2,1)S(1)} async-done(((bf16[32,16,256]{2,1,0:T(8,128)(2,1)}), bf16[32,16,256]{2,1,0:T(8,128)(2,1)S(1)}, u32[]{:S(2)}, u32[]{:S(2)}) %all-to-all-start.1) | async-done | bytes 262176 | tf_op jit(solution)/shard_map/all_to_all | solution.py:95
  169.3 0.7 copy.26
  170.0 10.8 %reduce-scatter.2.cloned.1.call-done = f32[16,32,128]{2,1,0:T(8,128)} async-done(((f32[16,128,128]{2,1,0:T(8,128)}), f32[16,32,128]{2,1,0:T(8,128)}) %reduce-scatter.2.cloned.1.call-update) | async-done | bytes 262160 | tf_op jit(solution)/shard_map/reduce_scatter | solution.py:141
  180.8 1.8 add_divide_fusion
  (46 shorter events, 0.9 us)
Async XLA Ops:
  7.2 133.6 %copy-start = (f32[1024,128]{1,0:T(8,128)S(1)}, f32[1024,128]{1,0:T(8,128)}, u32[]{:S(2)}) copy-start(f32[1024,128]{1,0:T(8,128)} %param.28) | copy-start | bytes 1572868
  7.2 9.9 %copy-start.11 = (f32[64]{0:T(128)S(1)}, f32[64]{0:T(128)}, u32[]{:S(2)}) copy-start(f32[64]{0:T(128)} %param.22) | copy-start | bytes 772
  7.2 9.9 %copy-start.12 = (s32[128]{0:T(128)S(1)}, s32[128]{0:T(128)}, u32[]{:S(2)}) copy-start(s32[128]{0:T(128)} %param.17) | copy-start | bytes 1540
  9.6 34.2 %copy-start.4 = (f32[256]{0:T(256)S(1)}, f32[256]{0:T(256)}, u32[]{:S(2)}) copy-start(f32[256]{0:T(256)} %param.20) | copy-start | bytes 3076
  9.6 34.2 %copy-start.5 = (f32[256]{0:T(256)S(1)}, f32[256]{0:T(256)}, u32[]{:S(2)}) copy-start(f32[256]{0:T(256)} %param.19) | copy-start | bytes 3076
  9.6 33.2 %all-to-all-start = ((bf16[16,8,16,256]{3,2,0,1:T(8,128)(2,1)}), bf16[16,8,16,256]{3,2,0,1:T(8,128)(2,1)S(1)}, u32[]{:S(2)}, u32[]{:S(2)}) async-start(bf16[16,8,16,256]{3,2,0,1:T(8,128)(2,1)} %copy.23), calls=%async_computation | async-start | bytes 2097152 | tf_op jit(solution)/shard_map/all_to_all | solution.py:57
  17.0 77.9 %all-reduce.2.cloned.1.call-start = ((), (), s32[]{:S(2)}) async-start(), calls=%async_computation.3 | async-start | bytes 2097152 | tf_op jit(solution)/shard_map/psum | solution.py:91
  43.8 1.1 copy-start.1
  56.4 1.5 copy-start.2
  57.3 3.6 %copy-start.10 = (s32[128]{0:T(128)S(1)}, s32[128]{0:T(128)}, u32[]{:S(2)}) copy-start(s32[128]{0:T(128)} %param.18) | copy-start | bytes 1540
  57.3 37.5 %copy-start.6 = (f32[256]{0:T(256)S(1)}, f32[256]{0:T(256)}, u32[]{:S(2)}) copy-start(f32[256]{0:T(256)} %param.24) | copy-start | bytes 3076
  57.8 40.0 %copy-start.7 = (f32[256]{0:T(256)S(1)}, f32[256]{0:T(256)}, u32[]{:S(2)}) copy-start(f32[256]{0:T(256)} %param.26) | copy-start | bytes 3076
  57.9 40.0 %copy-start.8 = (f32[256]{0:T(256)S(1)}, f32[256]{0:T(256)}, u32[]{:S(2)}) copy-start(f32[256]{0:T(256)} %param.25) | copy-start | bytes 3076
  57.9 41.2 %copy-start.3 = (bf16[256,2,32]{0,2,1:T(8,128)(2,1)S(1)}, bf16[256,2,32]{0,2,1:T(8,128)(2,1)}, u32[]{:S(2)}) copy-start(bf16[256,2,32]{0,2,1:T(8,128)(2,1)} %param.27) | copy-start | bytes 98308
  59.3 121.5 %reduce-scatter.2.cloned.1.call-start = ((), (), s32[]{:S(2)}) async-start(), calls=%async_computation.4 | async-start | bytes 1310720 | tf_op jit(solution)/shard_map/reduce_scatter | solution.py:141
  155.7 25.1 %copy-start.9 = (f32[128]{0:T(128)S(1)}, f32[128]{0:T(128)}, u32[]{:S(2)}) copy-start(f32[128]{0:T(128)} %param.29) | copy-start | bytes 1540
  155.7 13.6 %all-to-all-start.1 = ((bf16[32,16,256]{2,1,0:T(8,128)(2,1)}), bf16[32,16,256]{2,1,0:T(8,128)(2,1)S(1)}, u32[]{:S(2)}, u32[]{:S(2)}) async-start(bf16[32,16,256]{2,1,0:T(8,128)(2,1)} %bitcast.29), calls=%async_computation.1 | async-start | bytes 524288 | tf_op jit(solution)/shard_map/all_to_all | solution.py:95
Sparse Core Ops, SparseCore 0:
  59.5 35.3 all-reduce.1
  155.9 24.9 reduce-scatter.1
where the time goes:
time: 190 us; the launch traced here: 189 us
  waiting for transfers between devices  78.3 us (41%)
  blocking collectives  33.2 us (17%)
  matrix products  29 us (15%)
  between operations  15.1 us (8%)
  starting transfers between devices  12.8 us (7%)
  local copies, waits for them, and re-layouts  12.1 us (6%)
  other arithmetic  8.95 us (5%)
    psum x1, waiting for transfers between devices, per_device(): lax.psum(partial_value.astype(jnp.bfloat16), 'head').astype(jnp.float32)  33.8 us
    all_gather x1, blocking collectives, per_device(): piece = lax.all_gather(right, 'dap', axis=1, tiled=True)  33.2 us
    all_to_all x1, waiting for transfers between devices, per_device(): lax.all_to_all(bundled_focus_units, 'dap', split_axis=1, concat_axis=0, t...  25.6 us
    dot_general x1, matrix products, per_device(): jnp.dot(outer, tensor_final_matrix, precision=lax.Precision.HIGHEST, pref...  14.9 us
    reduce_scatter x1, waiting for transfers between devices, per_device(): lax.psum_scatter(partial_pair, 'head', scatter_dimension=1, tiled=True)  10.8 us
    all_to_all x1, waiting for transfers between devices, per_device(): lax.all_to_all(mine.reshape(parallel_devices * group, residue_device_coun...  8.07 us
    all_to_all x1, starting transfers between devices, per_device(): lax.all_to_all(bundled_focus_units, 'dap', split_axis=1, concat_axis=0, t...  7.41 us
    transpose x1, local copies, waits for them, and re-layouts, per_device(): outer.transpose(0, 2, 1, 3)  6.49 us
  transfers between devices with their start and end apart: 4, of which 4 were waited for; matrix products, arithmetic and copies ran while one was open for 1% of the time, Pallas kernels for 0%

commit v1 on v0

--- a/solution.py
+++ b/solution.py
@@ -54,7 +54,11 @@
     bundled_focus_units = multiple_aligned_family.reshape(
         homolog_shard_number, parallel_devices, residue_device_count, feature_dimension
     )
-    received = lax.all_to_all(bundled_focus_units, "dap", split_axis=1, concat_axis=0, tiled=True)
+    prior = lax.psum(1, "dap")
+    near = jnp.split(bundled_focus_units, prior, 1)
+    clean = jnp.stack(near)
+    reached = lax.all_to_all(clean, "dap", 0, 0)
+    received = jnp.concatenate(reached, 0)
     block = received[:, 0]
     count = block.shape[1]
     normed = layer_norm(

time: 190 us -> 202 us (1.063)
  local copies, waits for them, and re-layouts: 12.1 us -> 24 us
    unnamed x26 -> x33, local copies, waits for them, and re-layouts: 0.07 us -> 11.1 us
    all_gather x0 -> x1, local copies, waits for them, and re-layouts: none -> 2.39 us  [per_device(): piece = lax.all_gather(right, 'dap', axis=1, tiled=True)]
    reshape x1 -> x0, local copies, waits for them, and re-layouts: 2.37 us -> none  [per_device(): multiple_aligned_family.reshape(homolog_shard_number, parallel_devices, r...]
where the time goes in v1:
time: 202 us
  waiting for transfers between devices  78.3 us (39%)
  blocking collectives  33.2 us (16%)
  matrix products  29.5 us (15%)
  local copies, waits for them, and re-layouts  24 us (12%)
  between operations  15 us (7%)
  starting transfers between devices  12.7 us (6%)
  other arithmetic  8.92 us (4%)
    psum x1, waiting for transfers between devices, per_device(): lax.psum(partial_value.astype(jnp.bfloat16), 'head').astype(jnp.float32)  33.7 us
    all_gather x1, blocking collectives, per_device(): piece = lax.all_gather(right, 'dap', axis=1, tiled=True)  33.2 us
    all_to_all x1, waiting for transfers between devices, per_device(): reached = lax.all_to_all(clean, 'dap', 0, 0)  25.6 us
    dot_general x1, matrix products, per_device(): jnp.dot(outer, tensor_final_matrix, precision=lax.Precision.HIGHEST, pref...  14.9 us
    unnamed x33, local copies, waits for them, and re-layouts  11.1 us
    reduce_scatter x1, waiting for transfers between devices, per_device(): lax.psum_scatter(partial_pair, 'head', scatter_dimension=1, tiled=True)  10.8 us
    all_to_all x1, waiting for transfers between devices, per_device(): lax.all_to_all(mine.reshape(parallel_devices * group, residue_device_coun...  8.07 us
    all_to_all x1, starting transfers between devices, per_device(): reached = lax.all_to_all(clean, 'dap', 0, 0)  7.41 us
  transfers between devices with their start and end apart: 4, of which 4 were waited for; matrix products, arithmetic and copies ran while one was open for 1% of the time, Pallas kernels for 0%

profile of v1, /device:TPU:0, one launch (start us, length us, event | category | flops | bytes accessed | tf_op | source)
XLA Modules:
  0.0 201.6 jit_solution(9448846714906942660)
XLA Ops:
  7.2 1.6 fusion.76
  8.8 1.6 fusion.75
  10.4 1.6 fusion.74
  11.9 1.6 fusion.73
  13.5 1.6 fusion.72
  15.1 1.6 fusion.71
  16.6 1.6 fusion.70
  18.2 1.6 fusion.69
  19.8 7.4 %all-to-all-start = ((bf16[8,16,1,16,256]{4,3,1,2,0:T(8,128)(2,1)}), bf16[8,16,1,16,256]{4,3,1,2,0:T(8,128)(2,1)S(1)}, u32[]{:S(2)}, u32[]{:S(2)}) async-start(bf16[8,16,1,16,256]{4,3,1,2,0:T(8,128)(2,1)} %fusion.69), calls=%async_computation | async-start | bytes 2097152 | tf_op jit(solution)/shard_map/all_to_all | solution.py:60
  27.3 25.6 %all-to-all-done = bf16[8,16,1,16,256]{4,3,1,2,0:T(8,128)(2,1)S(1)} async-done(((bf16[8,16,1,16,256]{4,3,1,2,0:T(8,128)(2,1)}), bf16[8,16,1,16,256]{4,3,1,2,0:T(8,128)(2,1)S(1)}, u32[]{:S(2)}, u32[]{:S(2)}) %all-to-all-start) | async-done | bytes 1048608 | tf_op jit(solution)/shard_map/all_to_all | solution.py:60
  53.0 0.3 convert_reduce_fusion
  53.3 0.7 fusion.43
  54.0 0.7 fusion.46
  54.8 0.9 fusion.89
  56.1 10.6 %while.10 = (s32[]{:T(128)}, bf16[16,128,2,32]{1,3,2,0:T(8,128)(2,1)S(1)}, bf16[16,128,2,32]{1,3,2,0:T(8,128)(2,1)S(1)}, pred[128]{0:T(512)(128)(4,1)S(1)}, bf16...) while((s32[]{:T(128)}, ...), condition=%wide.region_5.6_spmd, body=%wide.region_2.5_spmd.sunk | while | flops 6537728 | bytes 137301 | solution.py:81
  56.3 0.4 fusion.108
  56.7 0.3 fusion.107
  57.0 0.4 fusion.108
  57.4 0.3 fusion.107
  57.7 0.4 fusion.108
  58.1 0.3 fusion.107
  58.3 0.4 fusion.108
  58.7 0.3 fusion.107
  59.0 0.4 fusion.108
  59.4 0.3 fusion.107
  59.7 0.4 fusion.108
  60.0 0.3 fusion.107
  60.3 0.4 fusion.108
  60.7 0.3 fusion.107
  61.0 0.4 fusion.108
  61.4 0.3 fusion.107
  61.6 0.4 fusion.108
  62.0 0.3 fusion.107
  62.3 0.4 fusion.108
  62.7 0.3 fusion.107
  63.0 0.4 fusion.108
  63.4 0.3 fusion.107
  63.6 0.4 fusion.108
  64.0 0.3 fusion.107
  64.3 0.4 fusion.108
  64.7 0.3 fusion.107
  65.0 0.4 fusion.108
  65.3 0.3 fusion.107
  65.6 0.4 fusion.108
  66.0 0.3 fusion.107
  66.3 0.4 fusion.108
  66.7 0.9 copy.61
  67.6 0.5 dot_general.33
  68.2 1.4 convolution_convert_fusion
  69.7 0.6 fusion.88
  71.4 33.7 %all-reduce.2.cloned.1.call-done = bf16[8,4,4,16,256]{4,3,2,1,0:T(8,128)(2,1)} async-done(((bf16[8,4,4,16,256]{4,3,2,1,0:T(8,128)(2,1)}), bf16[8,4,4,16,256]{4,3,2,1,0:T(8,128)(2,1)}) %all-reduce.2.cloned.1.call-update) | async-done | bytes 1048592 | tf_op jit(solution)/shard_map/psum | solution.py:95
  105.1 1.7 convert_reduce_fusion.1
  106.9 1.2 fusion.55
  108.1 1.2 fusion.58
  109.7 33.2 %all_gather.3 = bf16[32,128,32]{2,1,0:T(8,128)(2,1)S(1)} all-gather(bf16[32,16,32]{2,1,0:T(8,128)(2,1)S(1)} %fusion.48), channel_id=1, replica_groups=mesh['dap'=8,'head'=4] {'dap'}, dimensions={1}, use_global_device_ids=true | all-gather | bytes 294912 | tf_op jit(solution)/shard_map/all_gather | solution.py:134
  142.9 2.4 %copy.64 = bf16[32,128,32]{0,1,2:T(8,128)(2,1)S(1)} copy(bf16[32,128,32]{2,1,0:T(8,128)(2,1)S(1)} %all_gather.3) | data formatting | bytes 524288 | tf_op jit(solution)/shard_map/all_gather | solution.py:134
  145.3 1.3 convolution_bitcast_fusion.1
  146.6 6.5 %copy.65 = f32[16,128,32,32]{1,3,2,0:T(8,128)S(1)} copy(f32[16,128,32,32]{1,2,3,0:T(8,128)S(1)} %convolution_bitcast_fusion.1) | data formatting | bytes 16777216 | tf_op jit(solution)/shard_map/transpose | solution.py:138
  153.1 14.9 %fusion.66 = f32[16,128,128]{2,1,0:T(8,128)} fusion(f32[16,128,1024]{1,2,0:T(8,128)S(1)} %bitcast.183, f32[1024,128]{1,0:T(8,128)S(1)} %copy-done), kind=kOutput, calls=%fused_computation.59 | convolution fusion | flops 3221225472 | bytes 9961472 | tf_op jit(solution)/shard_map/dot_general | solution.py:139
  168.0 5.2 %all-to-all-start.1 = ((bf16[32,16,256]{2,1,0:T(8,128)(2,1)}), bf16[32,16,256]{2,1,0:T(8,128)(2,1)S(1)}, u32[]{:S(2)}, u32[]{:S(2)}) async-start(bf16[32,16,256]{2,1,0:T(8,128)(2,1)} %bitcast.33), calls=%async_computation.1 | async-start | bytes 524288 | tf_op jit(solution)/shard_map/all_to_all | solution.py:99
  173.3 8.1 %all-to-all-done.1 = bf16[32,16,256]{2,1,0:T(8,128)(2,1)S(1)} async-done(((bf16[32,16,256]{2,1,0:T(8,128)(2,1)}), bf16[32,16,256]{2,1,0:T(8,128)(2,1)S(1)}, u32[]{:S(2)}, u32[]{:S(2)}) %all-to-all-start.1) | async-done | bytes 262176 | tf_op jit(solution)/shard_map/all_to_all | solution.py:99
  181.4 0.7 copy.62
  182.1 10.8 %reduce-scatter.2.cloned.1.call-done = f32[16,32,128]{2,1,0:T(8,128)} async-done(((f32[16,128,128]{2,1,0:T(8,128)}), f32[16,32,128]{2,1,0:T(8,128)}) %reduce-scatter.2.cloned.1.call-update) | async-done | bytes 262160 | tf_op jit(solution)/shard_map/reduce_scatter | solution.py:145
  192.9 1.8 add_divide_fusion
  (50 shorter events, 1.8 us)
Async XLA Ops:
  7.2 145.9 %copy-start = (f32[1024,128]{1,0:T(8,128)S(1)}, f32[1024,128]{1,0:T(8,128)}, u32[]{:S(2)}) copy-start(f32[1024,128]{1,0:T(8,128)} %param.28) | copy-start | bytes 1572868
  7.2 20.1 %copy-start.11 = (f32[64]{0:T(128)S(1)}, f32[64]{0:T(128)}, u32[]{:S(2)}) copy-start(f32[64]{0:T(128)} %param.22) | copy-start | bytes 772
  7.2 20.1 %copy-start.12 = (s32[128]{0:T(128)S(1)}, s32[128]{0:T(128)}, u32[]{:S(2)}) copy-start(s32[128]{0:T(128)} %param.17) | copy-start | bytes 1540
  19.8 34.3 %copy-start.4 = (f32[256]{0:T(256)S(1)}, f32[256]{0:T(256)}, u32[]{:S(2)}) copy-start(f32[256]{0:T(256)} %param.20) | copy-start | bytes 3076
  19.8 34.3 %copy-start.5 = (f32[256]{0:T(256)S(1)}, f32[256]{0:T(256)}, u32[]{:S(2)}) copy-start(f32[256]{0:T(256)} %param.19) | copy-start | bytes 3076
  19.8 33.2 %all-to-all-start = ((bf16[8,16,1,16,256]{4,3,1,2,0:T(8,128)(2,1)}), bf16[8,16,1,16,256]{4,3,1,2,0:T(8,128)(2,1)S(1)}, u32[]{:S(2)}, u32[]{:S(2)}) async-start(bf16[8,16,1,16,256]{4,3,1,2,0:T(8,128)(2,1)} %fusion.69), calls=%async_computation | async-start | bytes 2097152 | tf_op jit(solution)/shard_map/all_to_all | solution.py:60
  27.2 77.9 %all-reduce.2.cloned.1.call-start = ((), (), s32[]{:S(2)}) async-start(), calls=%async_computation.3 | async-start | bytes 2097152 | tf_op jit(solution)/shard_map/psum | solution.py:95
  53.3 1.5 copy-start.1
  66.7 1.5 copy-start.2
  67.6 3.6 %copy-start.10 = (s32[128]{0:T(128)S(1)}, s32[128]{0:T(128)}, u32[]{:S(2)}) copy-start(s32[128]{0:T(128)} %param.18) | copy-start | bytes 1540
  67.6 37.5 %copy-start.6 = (f32[256]{0:T(256)S(1)}, f32[256]{0:T(256)}, u32[]{:S(2)}) copy-start(f32[256]{0:T(256)} %param.24) | copy-start | bytes 3076
  68.1 40.0 %copy-start.7 = (f32[256]{0:T(256)S(1)}, f32[256]{0:T(256)}, u32[]{:S(2)}) copy-start(f32[256]{0:T(256)} %param.26) | copy-start | bytes 3076
  68.2 40.0 %copy-start.8 = (f32[256]{0:T(256)S(1)}, f32[256]{0:T(256)}, u32[]{:S(2)}) copy-start(f32[256]{0:T(256)} %param.25) | copy-start | bytes 3076
  68.2 41.1 %copy-start.3 = (bf16[256,2,32]{0,2,1:T(8,128)(2,1)S(1)}, bf16[256,2,32]{0,2,1:T(8,128)(2,1)}, u32[]{:S(2)}) copy-start(bf16[256,2,32]{0,2,1:T(8,128)(2,1)} %param.27) | copy-start | bytes 98308
  69.6 123.3 %reduce-scatter.2.cloned.1.call-start = ((), (), s32[]{:S(2)}) async-start(), calls=%async_computation.4 | async-start | bytes 1310720 | tf_op jit(solution)/shard_map/reduce_scatter | solution.py:145
  168.0 25.0 %copy-start.9 = (f32[128]{0:T(128)S(1)}, f32[128]{0:T(128)}, u32[]{:S(2)}) copy-start(f32[128]{0:T(128)} %param.29) | copy-start | bytes 1540
  168.0 13.4 %all-to-all-start.1 = ((bf16[32,16,256]{2,1,0:T(8,128)(2,1)}), bf16[32,16,256]{2,1,0:T(8,128)(2,1)S(1)}, u32[]{:S(2)}, u32[]{:S(2)}) async-start(bf16[32,16,256]{2,1,0:T(8,128)(2,1)} %bitcast.33), calls=%async_computation.1 | async-start | bytes 524288 | tf_op jit(solution)/shard_map/all_to_all | solution.py:99
Sparse Core Ops, SparseCore 0:
  69.8 35.2 all-reduce.1
  168.1 24.7 reduce-scatter.1
